TPU v7x, 32 devices: a whole 2x2x4 slice. The times are simulated.
32 devices in a mesh: sec: 8 (over y, x, core), mpo: 4 (over z).
Axes of the slice: x: 2, y: 2, z: 4, core: 2. Of those that a mesh axis runs over, the one named last changes fastest.
Arguments:
- guess: float32 [6144, 256], P('sec'), may hold values from -6 to 6
- left_env: bfloat16 [20, 6144, 768], P('mpo', 'sec'), may hold values from -0.21875 to 0.21875
- right_env: bfloat16 [20, 2048, 256], P('mpo', 'sec'), may hold values from -0.375 to 0.375
- block_rows: int32 [8], replicated, may hold values from 1 to 768, 2048 in all
- charges: int32 [20], P('mpo'), may hold values from -2 to 2, as said below
- ranks: int32 [8], replicated, may hold values from 1 to 256
Outputs:
- wavefunction: float32 [6144, 256], P(('sec', 'mpo'))
- truncated: float32 [6144, 256], P(('sec', 'mpo'))
Inputs may be any that keep to these rules, and one draw needn't show every extreme that they name: The 5 terms of one index of mpo (each aligned run of 5 terms) carry the charges -2, -1, 0, 1, 2 once each.
All inputs are finite; a program needn't handle non-finite values.
Results may differ from a plain program's by a relative error of at most 0.01.
Values may be sent and summed in bfloat16 or wider, within the bound.
A program may use at most 64 MiB of HBM per device.

v0:
```python
import jax
import jax.numpy as jnp
from jax import lax
from jax.sharding import PartitionSpec as P

MEAN = 256
ITERS = 4


epsilon = 1e-06
step_size = 0.1
highest = lax.Precision.HIGHEST


def passed_along(array, axis, by):
    peers = lax.axis_size(axis)
    return lax.ppermute(array, axis, [(i, (i + by) % peers) for i in range(peers)])


def global_sum(values):
    totals = lax.psum(values, "sec")
    return totals


def apply_operator(current, left_env, right_env, charges, row_mask):
    rounded = current.astype(jnp.bfloat16)
    shifted = []
    for charge in (-2, -1, 0, 1, 2):
        if charge == 0:
            shifted.append(rounded)
        else:
            shifted.append(passed_along(rounded, "sec", charge))
    stacked = jnp.stack(shifted)
    inputs = jnp.take(stacked, charges + 2, axis=0)
    middle = jnp.einsum(
        "tij,tjk->tik", left_env, inputs, preferred_element_type=jnp.float32
    ).astype(jnp.bfloat16)
    summands = jnp.einsum("tik,tkl->til", middle, right_env, preferred_element_type=jnp.float32)
    applied = lax.psum(jnp.sum(summands, axis=0).astype(jnp.bfloat16), "mpo").astype(jnp.float32)
    return applied * row_mask


def shards(guess, left_env, right_env, block_rows, charges, ranks):
    capacity, right_width = guess.shape
    sectors = block_rows.shape[0]
    sector = lax.axis_index("sec")
    member = lax.axis_index("mpo")
    members = lax.axis_size("mpo")
    slab_rows = capacity // members
    entries = MEAN * sectors * right_width
    sector_ids = jnp.arange(sectors, dtype=jnp.int32)
    own_rows = jnp.sum(jnp.where(sector_ids == sector, block_rows, 0))
    own_rank = jnp.sum(jnp.where(sector_ids == sector, ranks, 0))
    current = guess
    row_mask = (jnp.arange(capacity, dtype=jnp.int32) < own_rows).astype(jnp.float32)[:, None]
    current = current * row_mask
    squares = global_sum((jnp.sum(current * current),))[0]
    current = current * lax.rsqrt(squares / entries + epsilon)
    for repeat in range(ITERS):
        applied = apply_operator(current, left_env, right_env, charges, row_mask)
        self_dot, cross_dot, image_dot = global_sum(
            (jnp.sum(current * current), jnp.sum(current * applied), jnp.sum(applied * applied))
        )
        rayleigh = cross_dot / (self_dot + epsilon)
        update = current - step_size * (applied - rayleigh * current)
        squares = self_dot * (1.0 - (step_size * rayleigh) ** 2) + step_size**2 * image_dot
        current = update * lax.rsqrt(squares / entries + epsilon)
    density = jnp.einsum("ij,ik->jk", current, current, precision=highest)
    slab = lax.dynamic_slice_in_dim(current, member * slab_rows, slab_rows, 0)
    columns = (jnp.arange(right_width, dtype=jnp.int32) < own_rank).astype(jnp.float32)
    span_basis = (jnp.eye(right_width, dtype=jnp.float32) + density / MEAN) * columns[None, :]
    gram_matrix = jnp.einsum("ij,ik->jk", span_basis, span_basis, precision=highest) + jnp.diag(
        1.0 - columns
    )
    factor = jnp.linalg.cholesky(gram_matrix)
    coords = jnp.einsum("ij,jk->ik", slab, span_basis, precision=highest)
    solved = jax.scipy.linalg.cho_solve((factor, True), coords.T).T
    truncated = jnp.einsum("ik,jk->ij", solved, span_basis, precision=highest)
    return (slab, truncated)


def solution(mesh):
    return jax.shard_map(
        shards,
        mesh=mesh,
        in_specs=(P("sec", None), P("mpo", "sec", None), P("mpo", "sec", None), P(), P("mpo"), P()),
        out_specs=(P(("sec", "mpo"), None), P(("sec", "mpo"), None)),
        check_vma=False,
    )
```

profile of v0, /device:TPU:25, one launch (start us, length us, event | category | flops | bytes accessed | tf_op | source)
XLA Modules:
  0.0 467.9 jit_solution(1288936652908784221)
XLA Ops:
  11.3 12.4 %psum.119 = f32[]{:T(128)} all-reduce(f32[]{:T(128)} %multiply_reduce_fusion.12), channel_id=1, replica_groups=mesh['sec'=8,'mpo'=4] {'sec'}, use_global_device_ids=true, to_apply=%region_2.3 | all-reduce | flops 1 | bytes 8 | tf_op jit(solution)/shard_map/psum | solution.py:21
  35.3 13.1 %collective-permute-done.1 = bf16[768,256]{1,0:T(8,128)(2,1)S(1)} collective-permute-done((bf16[768,256]{1,0:T(8,128)(2,1)S(1)}, bf16[768,256]{1,0:T(8,128)(2,1)S(1)}, u32[]{:S(2)}, u32[]{:S(2)}) %collective-permute-start.1) | collective-permute-done | bytes 393248 | tf_op jit(solution)/shard_map/ppermute | solution.py:17
  54.9 6.5 %fusion.75 = bf16[768,256]{1,0:T(8,128)(2,1)} fusion(bf16[5,256,256]{2,1,0:T(8,128)(2,1)S(1)} %copy-done, bf16[5,768,768]{2,1,0:T(8,128)(2,1)} %param.9, bf16[5,768,256]{2,1,0:T(8,128)(2,1)} %gather_fusion, pred[5]{0:T(512)(128)(4,1)S(1)} %get-tuple-element.47), kind=kOutput, calls=%fused_computation.37 | convolution fusion | flops 2015428608 | bytes 8912901 | tf_op jit(solution)/shard_map/tik,tkl->til/dot_general | solution.py:38
  61.4 35.0 %all-reduce.10.cloned.1.call-done = bf16[768,256]{1,0:T(8,128)(2,1)} async-done(((bf16[768,256]{1,0:T(8,128)(2,1)}), bf16[768,256]{1,0:T(8,128)(2,1)}) %all-reduce.10.cloned.1.call-update) | async-done | bytes 393232 | tf_op jit(solution)/shard_map/psum | solution.py:39
  98.4 14.4 %all-reduce.4 = (f32[]{:T(128)}, f32[]{:T(128)}, f32[]{:T(128)}) all-reduce(f32[]{:T(128)} %get-tuple-element.14, f32[]{:T(128)} %get-tuple-element.13, f32[]{:T(128)} %get-tuple-element.22), channel_id=1, replica_groups=mesh['sec'=8,'mpo'=4] {'sec'}, use_global_device_ids=true, to_apply=%region_7.9 | all-reduce | flops 3 | bytes 24 | tf_op jit(solution)/shard_map/psum | solution.py:21
  120.9 5.9 %collective-permute-done.4 = bf16[768,256]{1,0:T(8,128)(2,1)S(1)} collective-permute-done((bf16[768,256]{1,0:T(8,128)(2,1)S(1)}, bf16[768,256]{1,0:T(8,128)(2,1)S(1)}, u32[]{:S(2)}, u32[]{:S(2)}) %collective-permute-start.4) | collective-permute-done | bytes 393248 | tf_op jit(solution)/shard_map/ppermute | solution.py:17
  127.7 9.5 %collective-permute-done.5 = bf16[768,256]{1,0:T(8,128)(2,1)S(1)} collective-permute-done((bf16[768,256]{1,0:T(8,128)(2,1)S(1)}, bf16[768,256]{1,0:T(8,128)(2,1)S(1)}, u32[]{:S(2)}, u32[]{:S(2)}) %collective-permute-start.5) | collective-permute-done | bytes 393248 | tf_op jit(solution)/shard_map/ppermute | solution.py:17
  149.1 6.5 %fusion.70 = bf16[768,256]{1,0:T(8,128)(2,1)} fusion(bf16[5,256,256]{2,1,0:T(8,128)(2,1)S(1)} %copy-done, bf16[5,768,768]{2,1,0:T(8,128)(2,1)} %param.9, bf16[5,768,256]{2,1,0:T(8,128)(2,1)} %gather_fusion.1, pred[5]{0:T(512)(128)(4,1)S(1)} %get-tuple-element.47), kind=kOutput, calls=%fused_computation.36 | convolution fusion | flops 2015428608 | bytes 8912901 | tf_op jit(solution)/shard_map/tik,tkl->til/dot_general | solution.py:38
  155.6 33.8 %all-reduce.12.cloned.1.call-done = bf16[768,256]{1,0:T(8,128)(2,1)} async-done(((bf16[768,256]{1,0:T(8,128)(2,1)}), bf16[768,256]{1,0:T(8,128)(2,1)}) %all-reduce.12.cloned.1.call-update) | async-done | bytes 393232 | tf_op jit(solution)/shard_map/psum | solution.py:39
  191.4 14.4 %all-reduce.3 = (f32[]{:T(128)}, f32[]{:T(128)}, f32[]{:T(128)}) all-reduce(f32[]{:T(128)} %get-tuple-element.18, f32[]{:T(128)} %get-tuple-element.17, f32[]{:T(128)} %get-tuple-element.21), channel_id=1, replica_groups=mesh['sec'=8,'mpo'=4] {'sec'}, use_global_device_ids=true, to_apply=%region_14.16 | all-reduce | flops 3 | bytes 24 | tf_op jit(solution)/shard_map/psum | solution.py:21
  213.8 5.9 %collective-permute-done.8 = bf16[768,256]{1,0:T(8,128)(2,1)S(1)} collective-permute-done((bf16[768,256]{1,0:T(8,128)(2,1)S(1)}, bf16[768,256]{1,0:T(8,128)(2,1)S(1)}, u32[]{:S(2)}, u32[]{:S(2)}) %collective-permute-start.8) | collective-permute-done | bytes 393248 | tf_op jit(solution)/shard_map/ppermute | solution.py:17
  220.5 9.5 %collective-permute-done.9 = bf16[768,256]{1,0:T(8,128)(2,1)S(1)} collective-permute-done((bf16[768,256]{1,0:T(8,128)(2,1)S(1)}, bf16[768,256]{1,0:T(8,128)(2,1)S(1)}, u32[]{:S(2)}, u32[]{:S(2)}) %collective-permute-start.9) | collective-permute-done | bytes 393248 | tf_op jit(solution)/shard_map/ppermute | solution.py:17
  241.9 6.5 %fusion.65 = bf16[768,256]{1,0:T(8,128)(2,1)} fusion(bf16[5,256,256]{2,1,0:T(8,128)(2,1)S(1)} %copy-done, bf16[5,768,768]{2,1,0:T(8,128)(2,1)} %param.9, bf16[5,768,256]{2,1,0:T(8,128)(2,1)} %gather_fusion.2, pred[5]{0:T(512)(128)(4,1)S(1)} %get-tuple-element.47), kind=kOutput, calls=%fused_computation.35 | convolution fusion | flops 2015428608 | bytes 8912901 | tf_op jit(solution)/shard_map/tik,tkl->til/dot_general | solution.py:38
  248.5 33.8 %all-reduce.14.cloned.1.call-done = bf16[768,256]{1,0:T(8,128)(2,1)} async-done(((bf16[768,256]{1,0:T(8,128)(2,1)}), bf16[768,256]{1,0:T(8,128)(2,1)}) %all-reduce.14.cloned.1.call-update) | async-done | bytes 393232 | tf_op jit(solution)/shard_map/psum | solution.py:39
  284.5 14.6 %all-reduce.2 = (f32[]{:T(128)}, f32[]{:T(128)}, f32[]{:T(128)}) all-reduce(f32[]{:T(128)} %get-tuple-element.12, f32[]{:T(128)} %get-tuple-element.11, f32[]{:T(128)} %get-tuple-element.20), channel_id=1, replica_groups=mesh['sec'=8,'mpo'=4] {'sec'}, use_global_device_ids=true, to_apply=%region_21.23 | all-reduce | flops 3 | bytes 24 | tf_op jit(solution)/shard_map/psum | solution.py:21
  307.3 5.9 %collective-permute-done.12 = bf16[768,256]{1,0:T(8,128)(2,1)S(1)} collective-permute-done((bf16[768,256]{1,0:T(8,128)(2,1)S(1)}, bf16[768,256]{1,0:T(8,128)(2,1)S(1)}, u32[]{:S(2)}, u32[]{:S(2)}) %collective-permute-start.12) | collective-permute-done | bytes 393248 | tf_op jit(solution)/shard_map/ppermute | solution.py:17
  314.0 9.5 %collective-permute-done.13 = bf16[768,256]{1,0:T(8,128)(2,1)S(1)} collective-permute-done((bf16[768,256]{1,0:T(8,128)(2,1)S(1)}, bf16[768,256]{1,0:T(8,128)(2,1)S(1)}, u32[]{:S(2)}, u32[]{:S(2)}) %collective-permute-start.13) | collective-permute-done | bytes 393248 | tf_op jit(solution)/shard_map/ppermute | solution.py:17
  335.4 6.5 %fusion.60 = bf16[768,256]{1,0:T(8,128)(2,1)} fusion(bf16[5,256,256]{2,1,0:T(8,128)(2,1)S(1)} %copy-done, bf16[5,768,768]{2,1,0:T(8,128)(2,1)} %param.9, bf16[5,768,256]{2,1,0:T(8,128)(2,1)} %gather_fusion.3, pred[5]{0:T(512)(128)(4,1)S(1)} %get-tuple-element.47), kind=kOutput, calls=%fused_computation.34 | convolution fusion | flops 2015428608 | bytes 8912901 | tf_op jit(solution)/shard_map/tik,tkl->til/dot_general | solution.py:38
  343.9 31.9 %all-reduce.16.cloned.1.call-done = bf16[768,256]{1,0:T(8,128)(2,1)} async-done(((bf16[768,256]{1,0:T(8,128)(2,1)}), bf16[768,256]{1,0:T(8,128)(2,1)}) %all-reduce.16.cloned.1.call-update) | async-done | bytes 393232 | tf_op jit(solution)/shard_map/psum | solution.py:39
  377.8 14.4 %all-reduce.1 = (f32[]{:T(128)}, f32[]{:T(128)}, f32[]{:T(128)}) all-reduce(f32[]{:T(128)} %get-tuple-element.16, f32[]{:T(128)} %get-tuple-element.15, f32[]{:T(128)} %get-tuple-element.19), channel_id=1, replica_groups=mesh['sec'=8,'mpo'=4] {'sec'}, use_global_device_ids=true, to_apply=%region_28.30 | all-reduce | flops 3 | bytes 24 | tf_op jit(solution)/shard_map/psum | solution.py:21
  398.3 11.7 %cholesky.49 = f32[128,128]{1,0:T(8,128)S(1)} custom-call(f32[128,128]{1,0:T(8,128)S(1)} %cholesky.115), custom_call_target="Cholesky" | custom-call | tf_op jit(solution)/shard_map/jit(cholesky)/cholesky | solution.py:75
  410.1 9.8 %custom-call.18 = f32[1,128,128]{1,2,0:T(8,128)S(1)} custom-call(f32[1,128,128]{2,1,0:T(8,128)S(1)} %get-tuple-element.54), custom_call_target="InvertDiagBlocksLowerTriangular" | custom-call | tf_op jit(solution)/shard_map/jit(cholesky)/cholesky | solution.py:75
  420.4 11.9 %cholesky.103 = f32[128,128]{1,0:T(8,128)S(1)} custom-call(f32[128,128]{1,0:T(8,128)S(1)} %convolution_subtract_fusion.2), custom_call_target="Cholesky" | custom-call | tf_op jit(solution)/shard_map/jit(cholesky)/cholesky | solution.py:75
  438.4 19.7 %custom-call.19 = f32[2,128,128]{1,2,0:T(8,128)S(1)} custom-call(f32[2,128,128]{2,1,0:T(8,128)S(1)} %get-tuple-element.10), custom_call_target="InvertDiagBlocksLowerTriangular" | custom-call | tf_op jit(solution)/shard_map/jit(_cho_solve)/triangular_solve | solution.py:77
  (117 shorter events, 102.2 us)
Async XLA Ops:
  7.2 47.7 %copy-start = (bf16[5,256,256]{2,1,0:T(8,128)(2,1)S(1)}, bf16[5,256,256]{2,1,0:T(8,128)(2,1)}, u32[]{:S(2)}) copy-start(bf16[5,256,256]{2,1,0:T(8,128)(2,1)} %param.10) | copy-start | bytes 1966084
  7.2 41.2 %copy-start.1 = (f32[768,256]{1,0:T(8,128)S(1)}, f32[768,256]{1,0:T(8,128)}, u32[]{:S(2)}) copy-start(f32[768,256]{1,0:T(8,128)} %param.8) | copy-start | bytes 2359300
  7.2 22.9 %copy-start.4 = (s32[5]{0:T(128)S(1)}, s32[5]{0:T(128)}, u32[]{:S(2)}) copy-start(s32[5]{0:T(128)} %param.12) | copy-start | bytes 64
  7.2 89.2 %all-reduce.10.cloned.1.call-start = ((), (), s32[]{:S(2)}) async-start(), calls=%async_computation | async-start | bytes 786432 | tf_op jit(solution)/shard_map/psum | solution.py:39
  25.8 9.5 %collective-permute-start = (bf16[768,256]{1,0:T(8,128)(2,1)S(1)}, bf16[768,256]{1,0:T(8,128)(2,1)S(1)}, u32[]{:S(2)}, u32[]{:S(2)}) collective-permute-start(bf16[768,256]{1,0:T(8,128)(2,1)S(1)} %fusion.90), channel_id=1, source_target_pairs={{0,24},{4,28},{8,0},{12,4},{16,8},{20,12},{24,16},{28,20},{1,25},{... | collective-permute-start | bytes 1179656 | tf_op jit(solution)/shard_map/ppermute | solution.py:17
  27.4 20.9 %collective-permute-start.1 = (bf16[768,256]{1,0:T(8,128)(2,1)S(1)}, bf16[768,256]{1,0:T(8,128)(2,1)S(1)}, u32[]{:S(2)}, u32[]{:S(2)}) collective-permute-start(bf16[768,256]{1,0:T(8,128)(2,1)S(1)} %fusion.90), channel_id=1, source_target_pairs={{0,28},{4,0},{8,4},{12,8},{16,12},{20,16},{24,20},{28,24},{1,29},{... | collective-permute-start | bytes 1179656 | tf_op jit(solution)/shard_map/ppermute | solution.py:17
  28.4 20.2 %collective-permute-start.2 = (bf16[768,256]{1,0:T(8,128)(2,1)S(1)}, bf16[768,256]{1,0:T(8,128)(2,1)S(1)}, u32[]{:S(2)}, u32[]{:S(2)}) collective-permute-start(bf16[768,256]{1,0:T(8,128)(2,1)S(1)} %fusion.90), channel_id=1, source_target_pairs={{0,4},{4,8},{8,12},{12,16},{16,20},{20,24},{24,28},{28,0},{1,5},{5... | collective-permute-start | bytes 1179656 | tf_op jit(solution)/shard_map/ppermute | solution.py:17
  30.0 22.8 %collective-permute-start.3 = (bf16[768,256]{1,0:T(8,128)(2,1)S(1)}, bf16[768,256]{1,0:T(8,128)(2,1)S(1)}, u32[]{:S(2)}, u32[]{:S(2)}) collective-permute-start(bf16[768,256]{1,0:T(8,128)(2,1)S(1)} %fusion.90), channel_id=1, source_target_pairs={{0,8},{4,12},{8,16},{12,20},{16,24},{20,28},{24,0},{28,4},{1,9},{5... | collective-permute-start | bytes 1179656 | tf_op jit(solution)/shard_map/ppermute | solution.py:17
  61.4 128.0 %all-reduce.12.cloned.1.call-start = ((), (), s32[]{:S(2)}) async-start(), calls=%async_computation.1 | async-start | bytes 786432 | tf_op jit(solution)/shard_map/psum | solution.py:39
  116.8 10.1 %collective-permute-start.4 = (bf16[768,256]{1,0:T(8,128)(2,1)S(1)}, bf16[768,256]{1,0:T(8,128)(2,1)S(1)}, u32[]{:S(2)}, u32[]{:S(2)}) collective-permute-start(bf16[768,256]{1,0:T(8,128)(2,1)S(1)} %get-tuple-element.45), channel_id=1, source_target_pairs={{0,24},{4,28},{8,0},{12,4},{16,8},{20,12},{24,16},{28,20},{1,25},{... | collective-permute-start | bytes 1179656 | tf_op jit(solution)/shard_map/ppermute | solution.py:17
  117.3 19.9 %collective-permute-start.5 = (bf16[768,256]{1,0:T(8,128)(2,1)S(1)}, bf16[768,256]{1,0:T(8,128)(2,1)S(1)}, u32[]{:S(2)}, u32[]{:S(2)}) collective-permute-start(bf16[768,256]{1,0:T(8,128)(2,1)S(1)} %get-tuple-element.45), channel_id=1, source_target_pairs={{0,28},{4,0},{8,4},{12,8},{16,12},{20,16},{24,20},{28,24},{1,29},{... | collective-permute-start | bytes 1179656 | tf_op jit(solution)/shard_map/ppermute | solution.py:17
  118.2 20.6 %collective-permute-start.6 = (bf16[768,256]{1,0:T(8,128)(2,1)S(1)}, bf16[768,256]{1,0:T(8,128)(2,1)S(1)}, u32[]{:S(2)}, u32[]{:S(2)}) collective-permute-start(bf16[768,256]{1,0:T(8,128)(2,1)S(1)} %get-tuple-element.45), channel_id=1, source_target_pairs={{0,4},{4,8},{8,12},{12,16},{16,20},{20,24},{24,28},{28,0},{1,5},{5... | collective-permute-start | bytes 1179656 | tf_op jit(solution)/shard_map/ppermute | solution.py:17
  119.1 25.6 %collective-permute-start.7 = (bf16[768,256]{1,0:T(8,128)(2,1)S(1)}, bf16[768,256]{1,0:T(8,128)(2,1)S(1)}, u32[]{:S(2)}, u32[]{:S(2)}) collective-permute-start(bf16[768,256]{1,0:T(8,128)(2,1)S(1)} %get-tuple-element.45), channel_id=1, source_target_pairs={{0,8},{4,12},{8,16},{12,20},{16,24},{20,28},{24,0},{28,4},{1,9},{5... | collective-permute-start | bytes 1179656 | tf_op jit(solution)/shard_map/ppermute | solution.py:17
  155.6 126.7 %all-reduce.14.cloned.1.call-start = ((), (), s32[]{:S(2)}) async-start(), calls=%async_computation.2 | async-start | bytes 786432 | tf_op jit(solution)/shard_map/psum | solution.py:39
  209.6 10.1 %collective-permute-start.8 = (bf16[768,256]{1,0:T(8,128)(2,1)S(1)}, bf16[768,256]{1,0:T(8,128)(2,1)S(1)}, u32[]{:S(2)}, u32[]{:S(2)}) collective-permute-start(bf16[768,256]{1,0:T(8,128)(2,1)S(1)} %fusion.119), channel_id=1, source_target_pairs={{0,24},{4,28},{8,0},{12,4},{16,8},{20,12},{24,16},{28,20},{1,25},{... | collective-permute-start | bytes 1179656 | tf_op jit(solution)/shard_map/ppermute | solution.py:17
  210.1 19.9 %collective-permute-start.9 = (bf16[768,256]{1,0:T(8,128)(2,1)S(1)}, bf16[768,256]{1,0:T(8,128)(2,1)S(1)}, u32[]{:S(2)}, u32[]{:S(2)}) collective-permute-start(bf16[768,256]{1,0:T(8,128)(2,1)S(1)} %fusion.119), channel_id=1, source_target_pairs={{0,28},{4,0},{8,4},{12,8},{16,12},{20,16},{24,20},{28,24},{1,29},{... | collective-permute-start | bytes 1179656 | tf_op jit(solution)/shard_map/ppermute | solution.py:17
  211.0 20.6 %collective-permute-start.10 = (bf16[768,256]{1,0:T(8,128)(2,1)S(1)}, bf16[768,256]{1,0:T(8,128)(2,1)S(1)}, u32[]{:S(2)}, u32[]{:S(2)}) collective-permute-start(bf16[768,256]{1,0:T(8,128)(2,1)S(1)} %fusion.119), channel_id=1, source_target_pairs={{0,4},{4,8},{8,12},{12,16},{16,20},{20,24},{24,28},{28,0},{1,5},{5... | collective-permute-start | bytes 1179656 | tf_op jit(solution)/shard_map/ppermute | solution.py:17
  212.0 25.6 %collective-permute-start.11 = (bf16[768,256]{1,0:T(8,128)(2,1)S(1)}, bf16[768,256]{1,0:T(8,128)(2,1)S(1)}, u32[]{:S(2)}, u32[]{:S(2)}) collective-permute-start(bf16[768,256]{1,0:T(8,128)(2,1)S(1)} %fusion.119), channel_id=1, source_target_pairs={{0,8},{4,12},{8,16},{12,20},{16,24},{20,28},{24,0},{28,4},{1,9},{5... | collective-permute-start | bytes 1179656 | tf_op jit(solution)/shard_map/ppermute | solution.py:17
  241.9 40.4 %copy-start.2 = (bf16[768,256]{1,0:T(8,128)(2,1)S(1)}, bf16[768,256]{1,0:T(8,128)(2,1)}, u32[]{:S(2)}) copy-start(bf16[768,256]{1,0:T(8,128)(2,1)} %all-reduce.12.cloned.1.call-done) | copy-start | bytes 1179652
  248.5 127.3 %all-reduce.16.cloned.1.call-start = ((), (), s32[]{:S(2)}) async-start(), calls=%async_computation.3 | async-start | bytes 786432 | tf_op jit(solution)/shard_map/psum | solution.py:39
  303.1 10.1 %collective-permute-start.12 = (bf16[768,256]{1,0:T(8,128)(2,1)S(1)}, bf16[768,256]{1,0:T(8,128)(2,1)S(1)}, u32[]{:S(2)}, u32[]{:S(2)}) collective-permute-start(bf16[768,256]{1,0:T(8,128)(2,1)S(1)} %get-tuple-element.43), channel_id=1, source_target_pairs={{0,24},{4,28},{8,0},{12,4},{16,8},{20,12},{24,16},{28,20},{1,25},{... | collective-permute-start | bytes 1179656 | tf_op jit(solution)/shard_map/ppermute | solution.py:17
  303.6 19.9 %collective-permute-start.13 = (bf16[768,256]{1,0:T(8,128)(2,1)S(1)}, bf16[768,256]{1,0:T(8,128)(2,1)S(1)}, u32[]{:S(2)}, u32[]{:S(2)}) collective-permute-start(bf16[768,256]{1,0:T(8,128)(2,1)S(1)} %get-tuple-element.43), channel_id=1, source_target_pairs={{0,28},{4,0},{8,4},{12,8},{16,12},{20,16},{24,20},{28,24},{1,29},{... | collective-permute-start | bytes 1179656 | tf_op jit(solution)/shard_map/ppermute | solution.py:17
  304.5 20.6 %collective-permute-start.14 = (bf16[768,256]{1,0:T(8,128)(2,1)S(1)}, bf16[768,256]{1,0:T(8,128)(2,1)S(1)}, u32[]{:S(2)}, u32[]{:S(2)}) collective-permute-start(bf16[768,256]{1,0:T(8,128)(2,1)S(1)} %get-tuple-element.43), channel_id=1, source_target_pairs={{0,4},{4,8},{8,12},{12,16},{16,20},{20,24},{24,28},{28,0},{1,5},{5... | collective-permute-start | bytes 1179656 | tf_op jit(solution)/shard_map/ppermute | solution.py:17
  305.5 25.6 %collective-permute-start.15 = (bf16[768,256]{1,0:T(8,128)(2,1)S(1)}, bf16[768,256]{1,0:T(8,128)(2,1)S(1)}, u32[]{:S(2)}, u32[]{:S(2)}) collective-permute-start(bf16[768,256]{1,0:T(8,128)(2,1)S(1)} %get-tuple-element.43), channel_id=1, source_target_pairs={{0,8},{4,12},{8,16},{12,20},{16,24},{20,28},{24,0},{28,4},{1,9},{5... | collective-permute-start | bytes 1179656 | tf_op jit(solution)/shard_map/ppermute | solution.py:17
  (2 other events, 9.8 us)
Sparse Core Ops, SparseCore 0:
  61.5 34.8 all-reduce.9
  155.7 33.6 all-reduce.11
  248.6 33.6 all-reduce.13
  342.0 33.6 all-reduce.15
where the time goes:
time: 472 us; the launch traced here: 468 us
  waiting for transfers between devices  219 us (46%)
  other arithmetic  74.9 us (16%)
  blocking collectives  70.2 us (15%)
  matrix products  31.6 us (7%)
  local copies, waits for them, and re-layouts  28.9 us (6%)
  between operations  26.5 us (6%)
  starting transfers between devices  17 us (4%)
    psum x4, waiting for transfers between devices, apply_operator(): lax.psum(jnp.sum(summands, axis=0).astype(jnp.bfloat16), 'mpo')  134 us
    ppermute x16, waiting for transfers between devices, passed_along(): lax.ppermute(array, axis, [(i, (i + by) % peers) for i in range(peers)])  84.3 us
    psum x5, blocking collectives, global_sum(): totals = lax.psum(values, 'sec')  70.2 us
    another operation x6, other arithmetic, shards(): factor = jnp.linalg.cholesky(gram_matrix)  34.1 us
    dot_general x4, matrix products, apply_operator(): jnp.einsum('tik,tkl->til', middle, right_env, preferred_element_type=jnp....  25.9 us
    another operation x3, other arithmetic, shards(): solved = jax.scipy.linalg.cho_solve((factor, True), coords.T).T  19.7 us
    ppermute x16, starting transfers between devices, passed_along(): lax.ppermute(array, axis, [(i, (i + by) % peers) for i in range(peers)])  16.8 us
    gather x4, local copies, waits for them, and re-layouts, apply_operator(): inputs = jnp.take(stacked, charges + 2, axis=0)  12.9 us
  transfers between devices with their start and end apart: 20, of which 16 were waited for; matrix products, arithmetic and copies ran while one was open for 2% of the time, Pallas kernels for 0%

commit v1 on v0

v1 whole, which is shorter than its diff:
```python
import functools

import jax
import jax.numpy as jnp
from jax import lax
from jax.experimental import pallas as pl
from jax.experimental.pallas import tpu as pltpu
from jax.sharding import PartitionSpec as P

MEAN = 256
ITERS = 4


epsilon = 1e-06
step_size = 0.1
highest = lax.Precision.HIGHEST


def tile_sum(values):
    return jnp.sum(values.reshape(-1, 8, 128), axis=0)


def total(tile):
    return jnp.sum(jnp.sum(tile, axis=0, keepdims=True), axis=1, keepdims=True)


def iterate_kernel(
    sectors, members, entries,
    block_rows, charges, guess, left_hbm, right_hbm, out,
    left, right, xbuf, acc, app_chunk, cur, rs_out, rs_in, scal,
    load_sem, z_s, z_r, p_s, p_r, f_s, f_r, rs_s, rs_r, sc_s, sc_r,
):
    sector = lax.axis_index("sec")
    member = lax.axis_index("mpo")
    parity = lax.rem(sector, 2)
    capacity, width = guess.shape
    chunk = capacity // members
    terms = left.shape[0]
    sibling = sector + 1 - 2 * parity
    ahead = lax.rem(sector + 2, sectors)
    behind = lax.rem(sector + sectors - 2, sectors)
    sends = []

    loads = [
        pltpu.make_async_copy(left_hbm, left, load_sem.at[0]),
        pltpu.make_async_copy(right_hbm, right, load_sem.at[1]),
    ]
    for load in loads:
        load.start()

    barrier = pltpu.get_barrier_semaphore()
    for d in range(1, sectors):
        pl.semaphore_signal(
            barrier, inc=1, device_id=(lax.rem(sector + d, sectors), member),
            device_id_type=pl.DeviceIdType.MESH,
        )
    for d in range(1, members):
        pl.semaphore_signal(
            barrier, inc=1, device_id=(sector, lax.rem(member + d, members)),
            device_id_type=pl.DeviceIdType.MESH,
        )
    pl.semaphore_wait(barrier, sectors + members - 2)

    def remote(src, dst, send, recv, sec, mpo):
        return pltpu.make_async_remote_copy(
            src_ref=src, dst_ref=dst, send_sem=send, recv_sem=recv,
            device_id=(sec, mpo), device_id_type=pl.DeviceIdType.MESH,
        )

    def launch(copy):
        copy.start()
        sends.append(copy)

    def rows_of(j):
        return pl.ds(pl.multiple_of(j * chunk, chunk), chunk)

    def peer(d):
        return lax.rem(member + d, members)

    def z_copy(k, j, mpo):
        d = lax.rem(mpo - member + members, members)
        return remote(
            xbuf.at[k, 0, rows_of(j)], xbuf.at[k, 0, rows_of(j)],
            z_s.at[k, d], z_r.at[k, j], sector, mpo,
        )

    def plane_copy(k, j, slot):
        target = {1: sibling, 2: behind, 3: ahead}[slot]
        return remote(
            xbuf.at[k, 0, rows_of(j)], xbuf.at[k, slot, rows_of(j)],
            p_s.at[k, slot, j], p_r.at[k, slot, j], target, member,
        )

    def pass_copy(k, j):
        return remote(
            xbuf.at[k, 2 + parity, rows_of(j)], xbuf.at[k, 4, rows_of(j)],
            f_s.at[k, j], f_r.at[k, j], sibling, member,
        )

    def rs_copy(k, d):
        return remote(
            rs_out.at[k, d - 1], rs_in.at[k, d - 1],
            rs_s.at[k, d - 1], rs_r.at[k, d - 1], sector, peer(d),
        )

    def scal_copy(k, d):
        return remote(
            scal.at[k, sector], scal.at[k, sector],
            sc_s.at[k, d - 1], sc_r.at[k, d - 1], lax.rem(sector + d, sectors), member,
        )

    def scal_wait(k):
        for d in range(1, sectors):
            src = lax.rem(sector - d + sectors, sectors)
            remote(
                scal.at[k, src], scal.at[k, src],
                sc_s.at[k, d - 1], sc_r.at[k, d - 1], src, member,
            ).wait_recv()

    def plane_send(k, j):
        for slot in (2, 3, 1):
            launch(plane_copy(k, j, slot))

    def plane_wait(k, j, slot):
        remote(
            xbuf.at[k, slot, rows_of(j)], xbuf.at[k, slot, rows_of(j)],
            p_s.at[k, slot, j], p_r.at[k, slot, j], sibling, member,
        ).wait_recv()

    def other_wait(k, j):
        slot = 3 - parity
        remote(
            xbuf.at[k, slot, rows_of(j)], xbuf.at[k, slot, rows_of(j)],
            p_s.at[k, slot, j], p_r.at[k, slot, j], sibling, member,
        ).wait_recv()

    def passed_wait(k, j):
        slot = 2 + parity
        remote(
            xbuf.at[k, slot, rows_of(j)], xbuf.at[k, slot, rows_of(j)],
            p_s.at[k, slot, j], p_r.at[k, slot, j], sibling, member,
        ).wait_recv()

    def term_of(charge):
        index = jnp.int32(0)
        for i in range(1, terms):
            index = jnp.where(charges[i] == charge, i, index)
        return index

    slot_term = [
        term_of(0), term_of(2 * parity - 1), term_of(-2), term_of(2), term_of(1 - 2 * parity),
    ]

    def summand(k, slot, rows):
        index = slot_term[slot]
        middle = jnp.dot(
            left[index, rows, :], xbuf[k, slot], preferred_element_type=jnp.float32
        ).astype(jnp.bfloat16)
        return jnp.dot(middle, right[index], preferred_element_type=jnp.float32)

    def add_term(k, slot, first):
        def body(j, carry):
            rows = rows_of(j)
            value = summand(k, slot, rows)
            acc[rows, :] = value if first else acc[rows, :] + value
            return carry
        lax.fori_loop(0, members, body, 0)

    own_rows = block_rows[sector]
    order = [lax.rem(member + d, members) for d in range(members)]
    arrivals = [lax.rem(member - d + members, members) for d in range(members)]

    positions = lax.broadcasted_iota(jnp.int32, (capacity, width), 0)
    start = jnp.where(positions < own_rows, guess[...], 0.0)
    xbuf[0, 0] = start.astype(jnp.bfloat16)
    cur[...] = start
    for j in arrivals:
        plane_send(0, j)
    scal[0, sector, 0] = tile_sum(start * start)
    scal[0, sector, 1] = jnp.zeros((8, 128), jnp.float32)
    scal[0, sector, 2] = jnp.zeros((8, 128), jnp.float32)
    for d in range(1, sectors):
        launch(scal_copy(0, d))
    for load in loads:
        load.wait()

    def coefficients(k):
        sums = jnp.sum(scal[k], axis=0)
        if k == 0:
            scale = lax.rsqrt(total(sums[0]) / entries + epsilon)
            return scale, scale
        self_dot, cross_dot, image_dot = total(sums[0]), total(sums[1]), total(sums[2])
        rayleigh = cross_dot / (self_dot + epsilon)
        squares = self_dot * (1.0 - (step_size * rayleigh) ** 2) + step_size**2 * image_dot
        scale = lax.rsqrt(squares / entries + epsilon)
        return (1.0 + step_size * rayleigh) * scale, -step_size * scale

    for k in range(ITERS):
        last = k == ITERS - 1
        add_term(k, 0, True)
        for j in arrivals:
            plane_wait(k, j, 1)
        add_term(k, 1, False)
        for j in arrivals:
            passed_wait(k, j)
            launch(pass_copy(k, j))
        for j in arrivals:
            other_wait(k, j)
        add_term(k, 2, False)
        add_term(k, 3, False)
        for j in arrivals:
            remote(
                xbuf.at[k, 4, rows_of(j)], xbuf.at[k, 4, rows_of(j)],
                f_s.at[k, j], f_r.at[k, j], sibling, member,
            ).wait_recv()
        for d in range(1, members):
            rows = rows_of(order[d])
            rs_out[k, d - 1] = (acc[rows, :] + summand(k, 4, rows)).astype(jnp.bfloat16)
            launch(rs_copy(k, d))
        mine = rows_of(member)
        acc[mine, :] = acc[mine, :] + summand(k, 4, mine)
        scal_wait(k)
        keep, add = coefficients(k)
        for d in range(1, members):
            rs_copy(k, d).wait_recv()
        image = acc[mine, :]
        for d in range(1, members):
            image = image + rs_in[k, d - 1].astype(jnp.float32)
        positions = lax.broadcasted_iota(jnp.int32, (chunk, width), 0) + member * chunk
        image = jnp.where(positions < own_rows, image, 0.0) * add
        if k > 0:
            image = image + keep * app_chunk[...]
        app_chunk[...] = image
        xbuf[k + 1, 0, mine] = image.astype(jnp.bfloat16)
        for d in range(1, members):
            launch(z_copy(k + 1, member, order[d]))
        if not last:
            plane_send(k + 1, member)
        if k == 0:
            cur[...] = keep * cur[...]
        else:
            cur[...] = keep * cur[...] + add * xbuf[k, 0].astype(jnp.float32)
        for d in range(1, members):
            j = arrivals[d]
            remote(
                xbuf.at[k + 1, 0, rows_of(j)], xbuf.at[k + 1, 0, rows_of(j)],
                z_s.at[k + 1, d], z_r.at[k + 1, j], sector, order[d],
            ).wait_recv()
            if not last:
                plane_send(k + 1, j)
        state = cur[...]
        applied = xbuf[k + 1, 0].astype(jnp.float32)
        scal[k + 1, sector, 0] = tile_sum(state * state)
        scal[k + 1, sector, 1] = tile_sum(state * applied)
        scal[k + 1, sector, 2] = tile_sum(applied * applied)
        for d in range(1, sectors):
            launch(scal_copy(k + 1, d))
    scal_wait(ITERS)
    keep, add = coefficients(ITERS)
    out[...] = keep * cur[...] + add * xbuf[ITERS, 0].astype(jnp.float32)
    for copy in sends:
        copy.wait_send()


def iterate(guess, left_env, right_env, block_rows, charges):
    capacity, width = guess.shape
    terms = left_env.shape[0]
    sectors = lax.axis_size("sec")
    members = lax.axis_size("mpo")
    chunk = capacity // members
    entries = MEAN * sectors * width
    dma = pltpu.SemaphoreType.DMA
    vmem = pl.BlockSpec(memory_space=pltpu.VMEM)
    smem = pl.BlockSpec(memory_space=pltpu.SMEM)
    hbm = pl.BlockSpec(memory_space=pl.ANY)
    return pl.pallas_call(
        functools.partial(iterate_kernel, sectors, members, entries),
        out_shape=jax.ShapeDtypeStruct((capacity, width), jnp.float32),
        in_specs=[smem, smem, vmem, hbm, hbm],
        out_specs=vmem,
        scratch_shapes=[
            pltpu.VMEM(left_env.shape, left_env.dtype),
            pltpu.VMEM((terms, width, width), right_env.dtype),
            pltpu.VMEM((ITERS + 1, 5, capacity, width), jnp.bfloat16),
            pltpu.VMEM((capacity, width), jnp.float32),
            pltpu.VMEM((chunk, width), jnp.float32),
            pltpu.VMEM((capacity, width), jnp.float32),
            pltpu.VMEM((ITERS, members - 1, chunk, width), jnp.bfloat16),
            pltpu.VMEM((ITERS, members - 1, chunk, width), jnp.bfloat16),
            pltpu.VMEM((ITERS + 1, sectors, 3, 8, 128), jnp.float32),
            dma((2,)),
            dma((ITERS + 1, members)),
            dma((ITERS + 1, members)),
            dma((ITERS + 1, 5, members)),
            dma((ITERS + 1, 5, members)),
            dma((ITERS + 1, members)),
            dma((ITERS + 1, members)),
            dma((ITERS, members)),
            dma((ITERS, members)),
            dma((ITERS + 1, sectors)),
            dma((ITERS + 1, sectors)),
        ],
        compiler_params=pltpu.CompilerParams(
            collective_id=0, has_side_effects=True, vmem_limit_bytes=56 * 1024 * 1024
        ),
    )(block_rows, charges, guess, left_env, right_env)


def shards(guess, left_env, right_env, block_rows, charges, ranks):
    capacity, right_width = guess.shape
    sectors = block_rows.shape[0]
    sector = lax.axis_index("sec")
    member = lax.axis_index("mpo")
    members = lax.axis_size("mpo")
    slab_rows = capacity // members
    sector_ids = jnp.arange(sectors, dtype=jnp.int32)
    own_rank = jnp.sum(jnp.where(sector_ids == sector, ranks, 0))
    current = iterate(guess, left_env, right_env, block_rows, charges)
    density = jnp.einsum("ij,ik->jk", current, current, precision=highest)
    slab = lax.dynamic_slice_in_dim(current, member * slab_rows, slab_rows, 0)
    columns = (jnp.arange(right_width, dtype=jnp.int32) < own_rank).astype(jnp.float32)
    span_basis = (jnp.eye(right_width, dtype=jnp.float32) + density / MEAN) * columns[None, :]
    gram_matrix = jnp.einsum("ij,ik->jk", span_basis, span_basis, precision=highest) + jnp.diag(
        1.0 - columns
    )
    factor = jnp.linalg.cholesky(gram_matrix)
    coords = jnp.einsum("ij,jk->ik", slab, span_basis, precision=highest)
    solved = jax.scipy.linalg.cho_solve((factor, True), coords.T).T
    truncated = jnp.einsum("ik,jk->ij", solved, span_basis, precision=highest)
    return (slab, truncated)


def solution(mesh):
    return jax.shard_map(
        shards,
        mesh=mesh,
        in_specs=(P("sec", None), P("mpo", "sec", None), P("mpo", "sec", None), P(), P("mpo"), P()),
        out_specs=(P(("sec", "mpo"), None), P(("sec", "mpo"), None)),
        check_vma=False,
    )
```

time: 472 us -> 227 us (0.48)
  waiting for transfers between devices: 219 us -> 0 us
  Pallas kernels: 0 us -> 156 us
  blocking collectives: 70.2 us -> 0 us
  matrix products: 31.6 us -> 7.05 us
  between operations: 26.5 us -> 2.08 us
  local copies, waits for them, and re-layouts: 28.9 us -> 5.2 us
  other arithmetic: 74.9 us -> 56 us
  starting transfers between devices: 17 us -> 0 us
    pallas_call x0 -> x1, Pallas kernels: none -> 156 us  [iterate(): pl.pallas_call(functools.partial(iterate_kernel, sectors, members, entrie...]
    psum x4 -> x0, waiting for transfers between devices: 134 us -> none  [apply_operator(): lax.psum(jnp.sum(summands, axis=0).astype(jnp.bfloat16), 'mpo')]
    ppermute x16 -> x0, waiting for transfers between devices: 84.3 us -> none  [passed_along(): lax.ppermute(array, axis, [(i, (i + by) % peers) for i in range(peers)])]
    psum x5 -> x0, blocking collectives: 70.2 us -> none  [global_sum(): totals = lax.psum(values, 'sec')]
    dot_general x4 -> x0, matrix products: 25.9 us -> none  [apply_operator(): jnp.einsum('tik,tkl->til', middle, right_env, preferred_element_type=jnp....]
    ppermute x16 -> x0, starting transfers between devices: 16.8 us -> none  [passed_along(): lax.ppermute(array, axis, [(i, (i + by) % peers) for i in range(peers)])]
    gather x4 -> x0, local copies, waits for them, and re-layouts: 12.9 us -> none  [apply_operator(): inputs = jnp.take(stacked, charges + 2, axis=0)]
    reduce_sum x6 -> x0, other arithmetic: 11.6 us -> none  [the longest x4 8.22 us: shards(): jnp.sum(current * applied)]
  transfers between devices with their start and end apart: 20 -> 0, of which waited for: 16 -> 0; matrix products, arithmetic and copies ran while one was open for 2% -> 0% of each run, Pallas kernels for 0% -> 0%
where the time goes in v1:
time: 227 us
  Pallas kernels  156 us (69%)
  other arithmetic  56 us (25%)
  matrix products  7.05 us (3%)
  local copies, waits for them, and re-layouts  5.2 us (2%)
    pallas_call x1, Pallas kernels, iterate(): pl.pallas_call(functools.partial(iterate_kernel, sectors, members, entrie...  156 us
    another operation x6, other arithmetic, shards(): factor = jnp.linalg.cholesky(gram_matrix)  34.2 us
    another operation x3, other arithmetic, shards(): solved = jax.scipy.linalg.cho_solve((factor, True), coords.T).T  19.7 us

profile of v1, /device:TPU:25, one launch (start us, length us, event | category | flops | bytes accessed | tf_op | source)
XLA Modules:
  0.0 226.7 jit_solution(11311444885169849469)
XLA Ops:
  0.6 156.3 %shard_map.77 = f32[768,256]{1,0:T(8,128)} custom-call(s32[8]{0:T(128)} %block_rows.1, s32[5]{0:T(128)} %charges.1, f32[768,256]{1,0:T(8,128)} %guess.1, bf16[5,768,768]{2,1,0:T(8,128)(2,1)} %left_hbm.1, bf16[5,256,256]{2,1,0:T(8,128)(2,1)} %right_hbm.1), custom_call_target="tpu_custom_call" | custom-call | tf_op jit(solution)/shard_map/pallas_call | solution.py:276
  157.0 0.9 constant_dynamic-slice_fusion.1
  157.9 0.7 fusion.18
  158.6 0.6 compare_convert_fusion
  159.3 2.8 %fusion.1 = f32[256,256]{1,0:T(8,128)S(1)} fusion(f32[768,256]{1,0:T(8,128)} %shard_map.77, f32[256]{0:T(256)S(1)} %compare_convert_fusion), kind=kOutput, calls=%fused_computation.4 | convolution fusion | flops 604307456 | bytes 1049600 | tf_op jit(solution)/shard_map/ij,ik->jk/dot_general | solution.py:319
  162.1 0.3 fusion.22
  162.4 0.6 fusion.21
  163.2 0.6 broadcast_subtract_fusion
  163.9 11.7 %cholesky.49 = f32[128,128]{1,0:T(8,128)S(1)} custom-call(f32[128,128]{1,0:T(8,128)S(1)} %cholesky.115), custom_call_target="Cholesky" | custom-call | tf_op jit(solution)/shard_map/jit(cholesky)/cholesky | solution.py:326
  175.7 9.8 %custom-call.18 = f32[1,128,128]{1,2,0:T(8,128)S(1)} custom-call(f32[1,128,128]{2,1,0:T(8,128)S(1)} %get-tuple-element.23), custom_call_target="InvertDiagBlocksLowerTriangular" | custom-call | tf_op jit(solution)/shard_map/jit(cholesky)/cholesky | solution.py:326
  185.7 0.3 convolution_subtract_fusion.2
  186.0 11.9 %cholesky.103 = f32[128,128]{1,0:T(8,128)S(1)} custom-call(f32[128,128]{1,0:T(8,128)S(1)} %convolution_subtract_fusion.2), custom_call_target="Cholesky" | custom-call | tf_op jit(solution)/shard_map/jit(cholesky)/cholesky | solution.py:326
  197.9 0.7 compare_reduce_fusion
  200.0 4.1 %while.1 = (s32[]{:T(128)}, f32[256,256]{1,0:T(8,128)S(1)}, s32[2,2]{1,0:T(2,128)S(1)}, f32[2,128,128]{2,1,0:T(8,128)S(1)}, s32[]{:T(128)}) while((s32[]{:T(128)}, f32[256,256]{1,0:T(8,128)S(1)}, s32[2,2]{1,0:T(2,128)S(1)}, f32[2,128,128]{2,1,0:T(8,128)S(1)}, s32[]{:T(128)}) %tuple.27), condition=%wide.while_cond, body=%wide.while_body.sunk | while | flops 2 | bytes 131189 | solution.py:328
  200.1 0.7 fusion.38
  200.7 1.3 bitcast_dynamic-update-slice_fusion.2
  202.1 0.7 fusion.38
  202.8 1.3 bitcast_dynamic-update-slice_fusion.2
  204.1 19.7 %custom-call.19 = f32[2,128,128]{1,2,0:T(8,128)S(1)} custom-call(f32[2,128,128]{2,1,0:T(8,128)S(1)} %get-tuple-element.9), custom_call_target="InvertDiagBlocksLowerTriangular" | custom-call | tf_op jit(solution)/shard_map/jit(_cho_solve)/triangular_solve | solution.py:328
  224.0 0.3 convolution_subtract_fusion.1
  224.3 0.4 fusion.15
  224.7 0.4 fusion.14
  225.3 0.3 fusion.13
  225.6 1.1 fusion.4
  (19 shorter events, 1.1 us)
Async XLA Ops:
  0.6 157.3 %copy-start.1 = (s32[8]{0:T(128)S(1)}, s32[8]{0:T(128)}, u32[]{:S(2)}) copy-start(s32[8]{0:T(128)} %param.11) | copy-start | bytes 100
  157.9 68.8 %copy-start = (f32[192,256]{1,0:T(8,128)}, f32[192,256]{1,0:T(8,128)S(1)}, u32[]{:S(2)}) copy-start(f32[192,256]{1,0:T(8,128)S(1)} %constant_dynamic-slice_fusion.1) | copy-start | bytes 589828

commit v2 on v1

--- a/solution.py
+++ b/solution.py
@@ -306,6 +306,79 @@
     )(block_rows, charges, guess, left_env, right_env)
 
 
+BLOCK = 64
+
+
+def exact_dot(left, right, dims):
+    return lax.dot_general(
+        left, right, (dims, ((), ())), precision=highest, preferred_element_type=jnp.float32
+    )
+
+
+def inverse_factor(block):
+    rows = lax.broadcasted_iota(jnp.int32, (BLOCK, BLOCK), 0)
+    lanes = lax.broadcasted_iota(jnp.int32, (BLOCK, BLOCK), 1)
+    joined = jnp.concatenate([block, jnp.where(rows == lanes, 1.0, 0.0)], axis=1)
+    tiles = [joined[8 * i:8 * i + 8, :] for i in range(BLOCK // 8)]
+    below = lax.broadcasted_iota(jnp.int32, (8, 1), 0)
+    for j in range(BLOCK):
+        home, offset = divmod(j, 8)
+        row = tiles[home][offset:offset + 1, :]
+        scaled = row / row[:, j:j + 1]
+        for i in range(home, BLOCK // 8):
+            column = tiles[i][:, j:j + 1]
+            if i == home:
+                if offset == 7:
+                    continue
+                column = jnp.where(below > offset, column, 0.0)
+            tiles[i] = tiles[i] - column * scaled
+    joined = jnp.concatenate(tiles, axis=0)
+    wide_rows = lax.broadcasted_iota(jnp.int32, joined.shape, 0)
+    wide_lanes = lax.broadcasted_iota(jnp.int32, joined.shape, 1)
+    pivots = jnp.sum(jnp.where(wide_rows == wide_lanes, joined, 0.0), axis=1, keepdims=True)
+    return (joined * lax.rsqrt(pivots))[:, BLOCK:]
+
+
+def truncate_kernel(rank, density, slab, out, work, solved):
+    width = density.shape[0]
+    rows = lax.broadcasted_iota(jnp.int32, (width, width), 0)
+    lanes = lax.broadcasted_iota(jnp.int32, (width, width), 1)
+    identity = jnp.where(rows == lanes, 1.0, 0.0)
+    full = identity + density[...] / MEAN
+    kept = rank[0]
+    basis = jnp.where(lanes < kept, full, 0.0)
+    basis_t = jnp.where(rows < kept, full, 0.0)
+    work[:, :width] = exact_dot(basis_t, basis, ((1,), (0,))) + jnp.where(
+        rows < kept, 0.0, identity
+    )
+    work[:, width:] = basis_t
+    for first in range(0, width, BLOCK):
+        rest = first + BLOCK
+        inverse = inverse_factor(work[first:rest, first:rest])
+        reduced = exact_dot(inverse, work[first:rest, :], ((1,), (0,)))
+        solved[first:rest, :] = reduced[:, width:]
+        if rest < width:
+            column = exact_dot(work[rest:, first:rest], inverse, ((1,), (1,)))
+            work[rest:, :] = work[rest:, :] - exact_dot(column, reduced, ((1,), (0,)))
+    coords = exact_dot(slab[...], solved[...], ((1,), (1,)))
+    out[...] = exact_dot(coords, solved[...], ((1,), (0,)))
+
+
+def truncate(density, slab, rank):
+    width = density.shape[0]
+    vmem = pl.BlockSpec(memory_space=pltpu.VMEM)
+    return pl.pallas_call(
+        truncate_kernel,
+        out_shape=jax.ShapeDtypeStruct(slab.shape, jnp.float32),
+        in_specs=[pl.BlockSpec(memory_space=pltpu.SMEM), vmem, vmem],
+        out_specs=vmem,
+        scratch_shapes=[
+            pltpu.VMEM((width, 2 * width), jnp.float32),
+            pltpu.VMEM((width, width), jnp.float32),
+        ],
+    )(rank, density, slab)
+
+
 def shards(guess, left_env, right_env, block_rows, charges, ranks):
     capacity, right_width = guess.shape
     sectors = block_rows.shape[0]
@@ -318,15 +391,7 @@
     current = iterate(guess, left_env, right_env, block_rows, charges)
     density = jnp.einsum("ij,ik->jk", current, current, precision=highest)
     slab = lax.dynamic_slice_in_dim(current, member * slab_rows, slab_rows, 0)
-    columns = (jnp.arange(right_width, dtype=jnp.int32) < own_rank).astype(jnp.float32)
-    span_basis = (jnp.eye(right_width, dtype=jnp.float32) + density / MEAN) * columns[None, :]
-    gram_matrix = jnp.einsum("ij,ik->jk", span_basis, span_basis, precision=highest) + jnp.diag(
-        1.0 - columns
-    )
-    factor = jnp.linalg.cholesky(gram_matrix)
-    coords = jnp.einsum("ij,jk->ik", slab, span_basis, precision=highest)
-    solved = jax.scipy.linalg.cho_solve((factor, True), coords.T).T
-    truncated = jnp.einsum("ik,jk->ij", solved, span_basis, precision=highest)
+    truncated = truncate(density, slab, own_rank.reshape(1))
     return (slab, truncated)
 
 

time: 227 us -> 191 us (0.84)
  other arithmetic: 56 us -> 1.37 us
  Pallas kernels: 156 us -> 184 us
  local copies, waits for them, and re-layouts: 5.2 us -> 1.62 us
  matrix products: 7.05 us -> 3.49 us
    another operation x9 -> x0, other arithmetic: 53.9 us -> none  [the longest x6 34.2 us: shards(): factor = jnp.linalg.cholesky(gram_matrix)]
    pallas_call x0 -> x1, Pallas kernels: none -> 27.3 us  [truncate(): pl.pallas_call(truncate_kernel, out_shape=jax.ShapeDtypeStruct(slab.shape...]
    another operation x9 -> x0, local copies, waits for them, and re-layouts: 4.12 us -> none
where the time goes in v2:
time: 191 us
  Pallas kernels  184 us (96%)
  matrix products  3.49 us (2%)
    pallas_call x1, Pallas kernels, iterate(): pl.pallas_call(functools.partial(iterate_kernel, sectors, members, entrie...  156 us
    pallas_call x1, Pallas kernels, truncate(): pl.pallas_call(truncate_kernel, out_shape=jax.ShapeDtypeStruct(slab.shape...  27.3 us

profile of v2, /device:TPU:25, one launch (start us, length us, event | category | flops | bytes accessed | tf_op | source)
XLA Modules:
  0.0 190.8 jit_solution(7316745267591648064)
XLA Ops:
  0.6 1.4 fusion
  2.0 156.3 %shard_map.77 = f32[768,256]{1,0:T(8,128)} custom-call(s32[8]{0:T(128)} %block_rows.1, s32[5]{0:T(128)} %charges.1, f32[768,256]{1,0:T(8,128)} %guess.1, bf16[5,768,768]{2,1,0:T(8,128)(2,1)} %left_hbm.1, bf16[5,256,256]{2,1,0:T(8,128)(2,1)} %right_hbm.1), custom_call_target="tpu_custom_call" | custom-call | tf_op jit(solution)/shard_map/pallas_call | solution.py:276
  158.3 1.6 constant_dynamic-slice_fusion.slab
  159.9 3.5 %fusion.1.density = f32[256,256]{1,0:T(8,128)} fusion(f32[768,256]{1,0:T(8,128)} %shard_map.77), kind=kOutput, calls=%fused_computation.3 | convolution fusion | flops 603979776 | bytes 1048576 | tf_op jit(solution)/shard_map/ij,ik->jk/dot_general | solution.py:392
  163.4 27.3 %shard_map.78 = f32[192,256]{1,0:T(8,128)} custom-call(s32[1]{0:T(128)} %bitcast.rank, f32[256,256]{1,0:T(8,128)} %fusion.1.density, f32[192,256]{1,0:T(8,128)} %constant_dynamic-slice_fusion.slab), custom_call_target="tpu_custom_call" | custom-call | tf_op jit(solution)/shard_map/pallas_call | solution.py:370
